TPU v7x, 256 devices: a whole 4x4x8 slice. The times are simulated.
256 devices in a mesh: section: 8 (over y, x_lo), dev: 32 (over x_hi, z, core).
Axes of the slice: x: 4 (x_hi: 2, x_lo: 2; x = x_hi * 2 + x_lo), y: 4, z: 8, core: 2. Of those that a mesh axis runs over, the one named last changes fastest.
Arguments:
- patches: bfloat16 [8, 49152, 1280], P('section', 'dev'), may hold values from -6 to 6
- win_count: int32 [8, 32], P('section'), may hold values from 1 to 24, 256 in all within a row
- dest_perm: int32 [8, 32], P('section'), may hold values from 0 to 31, each once within a row
- win_groups: int32 [8, 32, 24], P('section'), may hold values from 2 to 16
- norm_gain: float32 [1280], replicated, may hold values from 0.5 to 1.5
- qkv_weight: bfloat16 [1280, 3840], P('dev')
- qkv_bias: float32 [3840], replicated, may hold values from -1.5 to 1.5
- proj_weight: bfloat16 [1280, 1280], P('dev'), may hold values from -0.15625 to 0.15625
- proj_bias: float32 [1280], replicated, may hold values from -1.5 to 1.5
- merge_gain: float32 [1280], replicated, may hold values from 0.5 to 1.5
- owner: int32 [8, 4096, 1], P('section', 'dev'), may hold values from 0 to 7; in each aligned block of 128 rows (0 to 127, 128 to 255, ..., all dimensions but the last counted through in order) at most 32 rows name the same one
Outputs:
- dispatched: bfloat16 [8, 8192, 5120], P('section', 'dev')
Inputs may be any that keep to these rules, and one draw needn't show every extreme that they name: `win_count`: within each section's row the counts sum to 8 times the devices of dev, and the largest is 24. `dest_perm`: each section's row is a permutation. `win_groups`: entries of slots past a device's count are not read. Among the 128 rows of one device, at most 32 have the same owner, and some device of every draw reaches 32.
All inputs are finite; a program needn't handle non-finite values.
Results may differ from a plain program's by a relative error of at most 0.0051.
Values may be sent and summed in bfloat16 or wider, within the bound.
No kernel may reach another device: no remote copies, remote signals or barrier semaphores. Data moves between devices by JAX's collectives and lax.ppermute only.
A program may use at most 128 MiB of HBM per device.

v0:
```python
import jax
import jax.numpy as jnp
from jax import lax
from jax.sharding import PartitionSpec as P

D = 1280
HEADS = 16
WIN = 64
DST_WIN = 8
SRC_WIN = 24


def normalize(values, gain):
    return values * lax.rsqrt(jnp.mean(values * values, axis=-1, keepdims=True) + 1e-06) * gain


def contract(inputs, shard):
    whole = lax.all_gather(shard, "dev", axis=0, tiled=True)
    return jnp.dot(inputs, whole, preferred_element_type=jnp.float32)


def encode(windows, groups, norm_gain, qkv_weight, qkv_bias, proj_weight, proj_bias, merge_gain):
    count = windows.shape[0]
    values = windows.reshape(count * WIN, D).astype(jnp.float32)
    normed = normalize(values, norm_gain).astype(jnp.bfloat16)
    triple = (contract(normed, qkv_weight) + qkv_bias).astype(jnp.bfloat16)
    triple = triple.reshape(count, WIN, 3, HEADS, D // HEADS)
    scores = jnp.einsum(
        "bqhe,bkhe->bhqk", triple[:, :, 0], triple[:, :, 1], preferred_element_type=jnp.float32
    )
    scores = scores * (D // HEADS) ** (-0.5)
    living = jnp.arange(WIN, dtype=jnp.int32)[None, :] < 4 * groups[:, None]
    scores = jnp.where(living[:, None, None, :], scores, -1e30)
    highest = jnp.max(scores, axis=-1, keepdims=True)
    powers = jnp.exp(scores - highest)
    probs = (powers / jnp.sum(powers, axis=-1, keepdims=True)).astype(jnp.bfloat16)
    mixed = jnp.einsum(
        "bhqk,bkhe->bqhe", probs, triple[:, :, 2], preferred_element_type=jnp.float32
    )
    mixed = mixed.astype(jnp.bfloat16).reshape(count * WIN, D)
    encoded = values + contract(mixed, proj_weight) + proj_bias
    final = normalize(encoded, merge_gain) * living.reshape(count * WIN, 1).astype(jnp.float32)
    return final.reshape(count * WIN // 4, 4 * D).astype(jnp.bfloat16)


def pack(merged, owners, section_count, capacity):
    sections = jnp.arange(section_count, dtype=jnp.int32)
    hits = (owners[:, None] == sections[None, :]).astype(jnp.int32)
    ranks = jnp.sum((jnp.cumsum(hits, axis=0) - hits) * hits, axis=1)
    places = owners * capacity + ranks
    chosen = places[None, :] == jnp.arange(section_count * capacity, dtype=jnp.int32)[:, None]
    ladder = jnp.arange(merged.shape[0], dtype=jnp.int32)
    indices = jnp.sum(chosen.astype(jnp.int32) * ladder[None, :], axis=1)
    filled = jnp.any(chosen, axis=1)
    return jnp.where(filled[:, None], merged[indices], jnp.zeros((), merged.dtype))


def body(
    patches,
    win_count,
    dest_perm,
    win_groups,
    norm_gain,
    qkv_weight,
    qkv_bias,
    proj_weight,
    proj_bias,
    merge_gain,
    owner,
):
    dev_count = lax.axis_size("dev")
    section_count = lax.axis_size("section")
    position = lax.axis_index("dev")
    windows = patches.reshape(SRC_WIN, WIN, D)
    counts = win_count[0]
    ladder = jnp.arange(dev_count, dtype=jnp.int32)
    before = jnp.sum(jnp.where(ladder[None, :] < ladder[:, None], counts[None, :], 0), axis=1)
    inverse = jnp.sum(
        ladder[:, None] * (dest_perm[0][:, None] == ladder[None, :]).astype(jnp.int32), axis=0
    )
    pair_slots = (SRC_WIN + dev_count - 1) // dev_count
    my_count = counts[position]
    begin_at = before[position]
    residue = jnp.mod(inverse - begin_at, dev_count)
    picked = jnp.arange(pair_slots, dtype=jnp.int32)[None, :] * dev_count + residue[:, None]
    usable = picked < my_count
    outgoing = jnp.where(
        usable[:, :, None, None],
        windows[jnp.minimum(picked, SRC_WIN - 1)],
        jnp.zeros((), windows.dtype),
    )
    outgoing = outgoing.reshape(dev_count * pair_slots * WIN, D)
    arrived = lax.all_to_all(outgoing, "dev", split_axis=0, concat_axis=0, tiled=True).reshape(
        dev_count, pair_slots, WIN, D
    )
    wanted = jnp.arange(DST_WIN, dtype=jnp.int32) * dev_count + inverse[position]
    source = jnp.sum((before[None, :] <= wanted[:, None]).astype(jnp.int32), axis=1) - 1
    within = wanted - before[source]
    balanced = arrived[source, within // dev_count]
    groups = win_groups[0][source, within]
    merged = encode(
        balanced, groups, norm_gain, qkv_weight, qkv_bias, proj_weight, proj_bias, merge_gain
    )
    merged_rows = merged.shape[0]
    capacity = 2 * merged_rows // section_count
    packed = pack(merged, owner[0, :, 0], section_count, capacity)
    delivered = lax.all_to_all(packed, "section", split_axis=0, concat_axis=0, tiled=True)
    return delivered.reshape(1, section_count * capacity, 4 * D)


def solution(mesh):
    return jax.shard_map(
        body,
        mesh=mesh,
        in_specs=(
            P("section", "dev", None),
            P("section", None),
            P("section", None),
            P("section", None, None),
            P(),
            P("dev", None),
            P(),
            P("dev", None),
            P(),
            P(),
            P("section", "dev", None),
        ),
        out_specs=P("section", "dev", None),
        check_vma=False,
    )
```

profile of v0, /device:TPU:1, one launch (start us, length us, event | category | flops | bytes accessed | tf_op | source)
XLA Modules:
  0.0 325.2 jit_solution(17619789578634482331)
XLA Ops:
  6.5 0.7 all-gather.3.cloned.1.call-update
  7.3 1.2 constant_dynamic-slice_fusion
  8.5 0.8 select_reduce_fusion.2
  9.9 0.7 select_reduce_fusion.3
  10.6 0.7 fusion.20
  11.3 5.3 %gather_fusion = bf16[32,64,1280]{2,1,0:T(8,128)(2,1)} fusion(bf16[24,64,1280]{2,1,0:T(8,128)(2,1)} %bitcast.76, s32[1024]{0:T(1024)S(1)} %pad_clamp_fusion.2), kind=kCustom, calls=%fused_computation | custom fusion | bytes 10485888 | tf_op jit(solution)/shard_map/gather | solution.py:89
  16.6 1.2 fusion.16
  17.8 5.2 %broadcast_select_fusion = bf16[32,64,1280]{2,1,0:T(8,128)(2,1)} fusion(bf16[32,64,1280]{2,1,0:T(8,128)(2,1)} %gather_fusion, pred[32]{0:T(512)(128)(4,1)S(1)} %fusion.16), kind=kLoop, calls=%fused_computation.7 | loop fusion | flops 2621440 | bytes 10485792 | tf_op jit(solution)/shard_map/jit(_where)/select_n | solution.py:87
  23.0 12.8 %all-to-all-start = ((bf16[32,64,1280]{2,1,0:T(8,128)(2,1)}), bf16[32,64,1280]{2,1,0:T(8,128)(2,1)}, u32[]{:S(2)}, u32[]{:S(2)}) async-start(bf16[32,64,1280]{2,1,0:T(8,128)(2,1)} %broadcast_select_fusion), calls=%async_computation | async-start | bytes 10485760 | tf_op jit(solution)/shard_map/all_to_all | solution.py:93
  35.8 0.7 all-gather.5.cloned.1.call-update
  37.1 0.6 multiply_add_fusion
  37.9 0.6 gather_fusion.1
  38.6 0.7 fusion.25
  39.3 0.6 gather_fusion.3
  40.9 138.5 %all-to-all-done = bf16[32,64,1280]{2,1,0:T(8,128)(2,1)} async-done(((bf16[32,64,1280]{2,1,0:T(8,128)(2,1)}), bf16[32,64,1280]{2,1,0:T(8,128)(2,1)}, u32[]{:S(2)}, u32[]{:S(2)}) %all-to-all-start) | async-done | bytes 5242912 | tf_op jit(solution)/shard_map/all_to_all | solution.py:93
  179.4 3.2 gather_fusion.2
  183.4 2.0 all-gather.3.cloned.1.call-done
  185.4 10.7 %add_convert_fusion = bf16[512,3840]{1,0:T(8,128)(2,1)} fusion(bf16[512,1280]{1,0:T(8,128)(2,1)S(1)} %fusion.4, bf16[1280,3840]{1,0:T(8,128)(2,1)} %all-gather.3.cloned.1.call-done, f32[3840]{0:T(1024)S(1)} %copy-done.5), kind=kOutput, calls=%fused_computation.6 | convolution fusion | flops 5037096960 | bytes 15088640 | tf_op jit(solution)/shard_map/dot_general | solution.py:19
  196.1 12.9 %reshape.324 = bf16[8,64,3,16,80]{4,3,2,1,0:T(8,128)(2,1)} reshape(bf16[512,3840]{1,0:T(8,128)(2,1)} %add_convert_fusion) | data formatting | bytes 7864320 | tf_op jit(solution)/shard_map/reshape | solution.py:27
  208.9 4.5 %fusion.30 = (bf16[8,64,1,16,80]{4,3,2,1,0:T(8,128)(2,1)S(1)}, bf16[8,64,1,16,80]{4,3,2,1,0:T(8,128)(2,1)S(1)}, bf16[8,64,1,16,80]{4,3,2,1,0:T(8,128)(2,1)S(1)}) fusion(bf16[8,64,3,16,80]{4,3,2,1,0:T(8,128)(2,1)} %reshape.324), kind=kLoop, calls=%fused_computation.86 | loop fusion | bytes 7864320 | tf_op jit(solution)/shard_map/slice | solution.py:38
  213.5 1.2 fusion.6
  214.7 2.3 fusion.31
  217.0 1.2 convert_bitcast_fusion
  218.2 1.4 copy.25
  219.6 3.3 %reshape.325 = bf16[512,1280]{1,0:T(8,128)(2,1)} reshape(bf16[8,64,16,80]{3,2,1,0:T(8,128)(2,1)S(1)} %copy.25) | data formatting | bytes 2621440 | tf_op jit(solution)/shard_map/reshape | solution.py:40
  222.9 47.1 %all-gather.5.cloned.1.call-done = bf16[1280,1280]{1,0:T(8,128)(2,1)} async-done(((bf16[40,1280]{1,0:T(8,128)(2,1)}), bf16[1280,1280]{1,0:T(8,128)(2,1)}) %all-gather.5.cloned.1.call-update) | async-done | bytes 3276816 | tf_op jit(solution)/shard_map/all_gather | solution.py:18
  270.0 4.4 %multiply_reduce_fusion = (f32[512]{0:T(512)S(1)}, f32[512,1280]{1,0:T(8,128)S(1)}) fusion(f32[1280]{0:T(1024)S(1)} %copy-done.6, bf16[512,1280]{1,0:T(8,128)(2,1)} %reshape.325, bf16[1280,1280]{1,0:T(8,128)(2,1)} %all-gather.5.cloned.1.call-done, bf16[512,1280]{1,0:T(8,128)(2,1)S(1)} %bitcast.73), kind=kOutput, calls=%fused_computation.18 | convolution fusion | flops 1680997888 | bytes 8526848 | tf_op jit(solution)/shard_map/dot_general | solution.py:19
  274.8 0.8 convert_element_type.62
  275.7 3.6 %gather_fusion.4 = bf16[256,5120]{1,0:T(8,128)(2,1)} fusion(bf16[128,5120]{1,0:T(8,128)(2,1)S(1)} %convert_element_type.62, s32[1024]{0:T(1024)S(1)} %pad_clamp_fusion), kind=kCustom, calls=%fused_computation.4 | custom fusion | bytes 5243904 | tf_op jit(solution)/shard_map/gather | solution.py:55
  279.2 2.0 broadcast_select_fusion.1
  281.2 35.6 %all_to_all.12 = bf16[8,32,5120]{2,1,0:T(8,128)(2,1)S(1)} all-to-all(bf16[8,32,5120]{2,1,0:T(8,128)(2,1)S(1)} %broadcast_select_fusion.1), channel_id=1, replica_groups=mesh['section'=8,'dev'=32] {'section'}, dimensions={0} | all-to-all | bytes 5242880 | tf_op jit(solution)/shard_map/all_to_all | solution.py:107
  316.9 1.5 copy.39
  (40 shorter events, 3.6 us)
Async XLA Ops:
  6.5 32.7 %copy-start = (s32[1,32,24]{1,2,0:T(8,128)S(1)}, s32[1,32,24]{1,2,0:T(8,128)}, u32[]{:S(2)}) copy-start(s32[1,32,24]{1,2,0:T(8,128)} %param.14) | copy-start | bytes 9220
  6.5 178.8 %all-gather.3.cloned.1.call-start = ((), (), s32[]{:S(2)}) async-start(), calls=%async_computation.2 | async-start | bytes 10137600 | tf_op jit(solution)/shard_map/all_gather | solution.py:18
  22.9 17.1 %copy-start.4 = (s32[1,128,1]{1,2,0:T(1,128)S(1)}, s32[1,128,1]{1,2,0:T(1,128)}, u32[]{:S(2)}) copy-start(s32[1,128,1]{1,2,0:T(1,128)} %param.21) | copy-start | bytes 1540
  23.0 156.4 %all-to-all-start = ((bf16[32,64,1280]{2,1,0:T(8,128)(2,1)}), bf16[32,64,1280]{2,1,0:T(8,128)(2,1)}, u32[]{:S(2)}, u32[]{:S(2)}) async-start(bf16[32,64,1280]{2,1,0:T(8,128)(2,1)} %broadcast_select_fusion), calls=%async_computation | async-start | bytes 10485760 | tf_op jit(solution)/shard_map/all_to_all | solution.py:93
  35.7 234.3 %all-gather.5.cloned.1.call-start = ((), (), s32[]{:S(2)}) async-start(), calls=%async_computation.3 | async-start | bytes 3379200 | tf_op jit(solution)/shard_map/all_gather | solution.py:18
  37.9 145.1 %copy-start.2 = (f32[1280]{0:T(1024)S(1)}, f32[1280]{0:T(1024)}, u32[]{:S(2)}) copy-start(f32[1280]{0:T(1024)} %param.15) | copy-start | bytes 15364
  182.6 2.8 copy-start.5
  219.6 50.4 %copy-start.6 = (f32[1280]{0:T(1024)S(1)}, f32[1280]{0:T(1024)}, u32[]{:S(2)}) copy-start(f32[1280]{0:T(1024)} %param.19) | copy-start | bytes 15364
  270.0 4.4 %copy-start.3 = (f32[1280]{0:T(1024)S(1)}, f32[1280]{0:T(1024)}, u32[]{:S(2)}) copy-start(f32[1280]{0:T(1024)} %param.20) | copy-start | bytes 15364
  316.9 1.5 copy-start.1
Sparse Core Ops, SparseCore 0:
  10.0 175.2 all-gather.2
  188.1 81.9 all-gather.4
where the time goes:
time: 326 us; the launch traced here: 325 us
  waiting for transfers between devices  189 us (58%)
  local copies, waits for them, and re-layouts  40.5 us (12%)
  blocking collectives  35.6 us (11%)
  matrix products  17.5 us (5%)
  other arithmetic  16.2 us (5%)
  between operations  13.6 us (4%)
  starting transfers between devices  12.8 us (4%)
    all_to_all x1, waiting for transfers between devices, body(): lax.all_to_all(outgoing, 'dev', split_axis=0, concat_axis=0, tiled=True)  138 us
    all_gather x2, waiting for transfers between devices, contract(): whole = lax.all_gather(shard, 'dev', axis=0, tiled=True)  49.1 us
    all_to_all x1, blocking collectives, body(): lax.all_to_all(packed, 'section', split_axis=0, concat_axis=0, tiled=True)  35.6 us
    dot_general x2, matrix products, contract(): return jnp.dot(inputs, whole, preferred_element_type=jnp.float32)  15 us
    reshape x1, local copies, waits for them, and re-layouts, encode(): triple = triple.reshape(count, WIN, 3, HEADS, D // HEADS)  12.9 us
    all_to_all x1, starting transfers between devices, body(): lax.all_to_all(outgoing, 'dev', split_axis=0, concat_axis=0, tiled=True)  12.8 us
  transfers between devices with their start and end apart: 3, of which 3 were waited for; matrix products, arithmetic and copies ran while one was open for 19% of the time, Pallas kernels for 0%

commit v1 on v0

--- a/solution.py
+++ b/solution.py
@@ -15,7 +15,9 @@
 
 
 def contract(inputs, shard):
-    whole = lax.all_gather(shard, "dev", axis=0, tiled=True)
+    whole = jnp.concatenate(
+        lax.all_to_all(jnp.stack([shard] * lax.axis_size("dev")), "dev", 0, 0), axis=0
+    )
     return jnp.dot(inputs, whole, preferred_element_type=jnp.float32)
 
 

time: 326 us -> 510 us (1.56)
  blocking collectives: 35.6 us -> 166 us
  waiting for transfers between devices: 189 us -> 247 us
  between operations: 13.6 us -> 0.25 us
  local copies, waits for them, and re-layouts: 40.5 us -> 46.8 us
  starting transfers between devices: 12.8 us -> 18.2 us
    all_to_all x0 -> x1, blocking collectives: none -> 130 us  [body(): lax.all_to_all(outgoing, 'dev', split_axis=0, concat_axis=0, tiled=True)]
    all_to_all x1 -> x2, waiting for transfers between devices: 138 us -> 247 us  [contract(): lax.all_to_all(jnp.stack([shard] * lax.axis_size('dev')), 'dev', 0, 0)]
    all_gather x2 -> x0, waiting for transfers between devices: 49.1 us -> none  [contract(): whole = lax.all_gather(shard, 'dev', axis=0, tiled=True)]
    another operation x0 -> x2, local copies, waits for them, and re-layouts: none -> 6.41 us  [contract(): jnp.stack([shard] * lax.axis_size('dev'))]
    all_to_all x1 -> x2, starting transfers between devices: 12.8 us -> 18.2 us  [contract(): lax.all_to_all(jnp.stack([shard] * lax.axis_size('dev')), 'dev', 0, 0)]
  transfers between devices with their start and end apart: 3 -> 2, of which waited for: 3 -> 2; matrix products, arithmetic and copies ran while one was open for 19% -> 9% of each run, Pallas kernels for 0% -> 0%
where the time goes in v1:
time: 510 us; the launch traced here: 509 us
  waiting for transfers between devices  247 us (48%)
  blocking collectives  166 us (33%)
  local copies, waits for them, and re-layouts  46.8 us (9%)
  starting transfers between devices  18.2 us (4%)
  matrix products  17.5 us (3%)
  other arithmetic  14.1 us (3%)
    all_to_all x2, waiting for transfers between devices, contract(): lax.all_to_all(jnp.stack([shard] * lax.axis_size('dev')), 'dev', 0, 0)  247 us
    all_to_all x1, blocking collectives, body(): lax.all_to_all(outgoing, 'dev', split_axis=0, concat_axis=0, tiled=True)  130 us
    all_to_all x1, blocking collectives, body(): lax.all_to_all(packed, 'section', split_axis=0, concat_axis=0, tiled=True)  35.4 us
    all_to_all x2, starting transfers between devices, contract(): lax.all_to_all(jnp.stack([shard] * lax.axis_size('dev')), 'dev', 0, 0)  18.2 us
    dot_general x2, matrix products, contract(): return jnp.dot(inputs, whole, preferred_element_type=jnp.float32)  15.1 us
    reshape x1, local copies, waits for them, and re-layouts, encode(): triple = triple.reshape(count, WIN, 3, HEADS, D // HEADS)  12.9 us
  transfers between devices with their start and end apart: 2, of which 2 were waited for; matrix products, arithmetic and copies ran while one was open for 9% of the time, Pallas kernels for 0%

profile of v1, /device:TPU:1, one launch (start us, length us, event | category | flops | bytes accessed | tf_op | source)
XLA Modules:
  0.0 509.5 jit_solution(13662664592954651617)
XLA Ops:
  0.0 0.8 select_reduce_fusion.3
  0.8 0.8 select_reduce_fusion.2
  1.5 1.3 constant_dynamic-slice_fusion
  3.4 0.7 fusion.18
  4.1 1.3 fusion.14
  5.5 5.3 %gather_fusion = bf16[32,64,1280]{2,1,0:T(8,128)(2,1)} fusion(bf16[24,64,1280]{2,1,0:T(8,128)(2,1)} %bitcast.75, s32[1024]{0:T(1024)S(1)} %pad_clamp_fusion.2), kind=kCustom, calls=%fused_computation | custom fusion | bytes 10485888 | tf_op jit(solution)/shard_map/gather | solution.py:91
  10.8 2.9 broadcast_select_fusion
  13.7 130.2 %all_to_all.22 = bf16[32,64,1280]{2,1,0:T(8,128)(2,1)} all-to-all(bf16[32,64,1280]{2,1,0:T(8,128)(2,1)S(1)} %broadcast_select_fusion), channel_id=1, replica_groups=mesh['section'=8,'dev'=32] {'dev'}, dimensions={0} | all-to-all | bytes 10485760 | tf_op jit(solution)/shard_map/all_to_all | solution.py:95
  143.9 4.4 stack.4
  148.3 7.1 %all-to-all-start.1 = ((bf16[32,40,3840]{2,1,0:T(8,128)(2,1)}), bf16[32,40,3840]{2,1,0:T(8,128)(2,1)}, u32[]{:S(2)}, u32[]{:S(2)}) async-start(bf16[32,40,3840]{2,1,0:T(8,128)(2,1)} %stack.4), calls=%async_computation.1 | async-start | bytes 19660800 | tf_op jit(solution)/shard_map/all_to_all | solution.py:19
  156.0 0.6 multiply_add_fusion
  156.8 214.9 %all-to-all-done.1 = bf16[32,40,3840]{2,1,0:T(8,128)(2,1)} async-done(((bf16[32,40,3840]{2,1,0:T(8,128)(2,1)}), bf16[32,40,3840]{2,1,0:T(8,128)(2,1)}, u32[]{:S(2)}, u32[]{:S(2)}) %all-to-all-start.1) | async-done | bytes 9830432 | tf_op jit(solution)/shard_map/all_to_all | solution.py:19
  371.7 2.0 stack.5
  373.7 11.1 %all-to-all-start.2 = ((bf16[32,40,1280]{2,1,0:T(8,128)(2,1)}), bf16[32,40,1280]{2,1,0:T(8,128)(2,1)}, u32[]{:S(2)}, u32[]{:S(2)}) async-start(bf16[32,40,1280]{2,1,0:T(8,128)(2,1)} %stack.5), calls=%async_computation.2 | async-start | bytes 6553600 | tf_op jit(solution)/shard_map/all_to_all | solution.py:19
  384.9 0.6 gather_fusion.1
  385.6 0.7 fusion.23
  387.9 3.1 gather_fusion.2
  391.7 10.7 %add_convert_fusion = bf16[512,3840]{1,0:T(8,128)(2,1)} fusion(bf16[512,1280]{1,0:T(8,128)(2,1)S(1)} %bitcast.76, bf16[1280,3840]{1,0:T(8,128)(2,1)} %bitcast.17, f32[3840]{0:T(1024)S(1)} %copy-done.7), kind=kOutput, calls=%fused_computation.6 | convolution fusion | flops 5037096960 | bytes 15088640 | tf_op jit(solution)/shard_map/dot_general | solution.py:21
  402.4 12.9 %reshape.376 = bf16[8,64,3,16,80]{4,3,2,1,0:T(8,128)(2,1)} reshape(bf16[512,3840]{1,0:T(8,128)(2,1)} %add_convert_fusion) | data formatting | bytes 7864320 | tf_op jit(solution)/shard_map/reshape | solution.py:29
  415.3 4.5 fusion.28
  419.8 1.2 fusion.4
  421.1 2.3 fusion.29
  423.4 1.2 convert_bitcast_fusion
  424.6 1.4 copy.25
  426.0 3.3 reshape.377
  429.3 32.1 %all-to-all-done.2 = bf16[32,40,1280]{2,1,0:T(8,128)(2,1)} async-done(((bf16[32,40,1280]{2,1,0:T(8,128)(2,1)}), bf16[32,40,1280]{2,1,0:T(8,128)(2,1)}, u32[]{:S(2)}, u32[]{:S(2)}) %all-to-all-start.2) | async-done | bytes 3276832 | tf_op jit(solution)/shard_map/all_to_all | solution.py:19
  461.4 4.4 multiply_reduce_fusion
  466.2 0.8 convert_element_type.79
  467.0 3.6 gather_fusion.4
  470.6 2.0 broadcast_select_fusion.1
  472.5 35.4 %all_to_all.23 = bf16[8,32,5120]{2,1,0:T(8,128)(2,1)S(1)} all-to-all(bf16[8,32,5120]{2,1,0:T(8,128)(2,1)S(1)} %broadcast_select_fusion.1), channel_id=1, replica_groups=mesh['section'=8,'dev'=32] {'section'}, dimensions={0} | all-to-all | bytes 5242880 | tf_op jit(solution)/shard_map/all_to_all | solution.py:109
  508.0 1.5 copy.39
  (42 shorter events, 4.1 us)
Async XLA Ops:
  0.0 386.2 %copy-start = (s32[1,32,24]{1,2,0:T(8,128)S(1)}, s32[1,32,24]{1,2,0:T(8,128)}, u32[]{:S(2)}) copy-start(s32[1,32,24]{1,2,0:T(8,128)} %param.14) | copy-start | bytes 9220
  13.7 130.3 %copy-start.2 = (bf16[40,3840]{1,0:T(8,128)(2,1)S(1)}, bf16[40,3840]{1,0:T(8,128)(2,1)}, u32[]{:S(2)}) copy-start(bf16[40,3840]{1,0:T(8,128)(2,1)} %param.16) | copy-start | bytes 921604
  148.3 223.4 %copy-start.3 = (bf16[40,1280]{1,0:T(8,128)(2,1)S(1)}, bf16[40,1280]{1,0:T(8,128)(2,1)}, u32[]{:S(2)}) copy-start(bf16[40,1280]{1,0:T(8,128)(2,1)} %param.18) | copy-start | bytes 307204
  148.3 223.4 %all-to-all-start.1 = ((bf16[32,40,3840]{2,1,0:T(8,128)(2,1)}), bf16[32,40,3840]{2,1,0:T(8,128)(2,1)}, u32[]{:S(2)}, u32[]{:S(2)}) async-start(bf16[32,40,3840]{2,1,0:T(8,128)(2,1)} %stack.4), calls=%async_computation.1 | async-start | bytes 19660800 | tf_op jit(solution)/shard_map/all_to_all | solution.py:19
  373.7 13.3 %copy-start.6 = (s32[1,128,1]{1,2,0:T(1,128)S(1)}, s32[1,128,1]{1,2,0:T(1,128)}, u32[]{:S(2)}) copy-start(s32[1,128,1]{1,2,0:T(1,128)} %param.21) | copy-start | bytes 1540
  373.7 87.6 %all-to-all-start.2 = ((bf16[32,40,1280]{2,1,0:T(8,128)(2,1)}), bf16[32,40,1280]{2,1,0:T(8,128)(2,1)}, u32[]{:S(2)}, u32[]{:S(2)}) async-start(bf16[32,40,1280]{2,1,0:T(8,128)(2,1)} %stack.5), calls=%async_computation.2 | async-start | bytes 6553600 | tf_op jit(solution)/shard_map/all_to_all | solution.py:19
  384.9 6.4 %copy-start.4 = (f32[1280]{0:T(1024)S(1)}, f32[1280]{0:T(1024)}, u32[]{:S(2)}) copy-start(f32[1280]{0:T(1024)} %param.15) | copy-start | bytes 15364
  391.0 0.7 copy-start.7
  425.9 35.4 %copy-start.8 = (f32[1280]{0:T(1024)S(1)}, f32[1280]{0:T(1024)}, u32[]{:S(2)}) copy-start(f32[1280]{0:T(1024)} %param.19) | copy-start | bytes 15364
  461.4 4.4 copy-start.5
  508.0 1.5 copy-start.1
